TPU v7x, 32 devices: a whole 2x2x4 slice. The times are simulated.
32 devices in a mesh: tile: 8 (over z, y), chan: 4 (over x, core).
Axes of the slice: x: 2, y: 2, z: 4, core: 2. Of those that a mesh axis runs over, the one named last changes fastest.
Arguments:
- feat: bfloat16 [128, 64, 256], P('tile', 'chan'), may hold values from -6 to 6
- lift: float32 [64], replicated, may hold values from -3 to 3
- dilation4_weight: bfloat16 [3, 3, 64, 64], replicated, may hold values from -0.25 to 0.25
- dilation8_weight: bfloat16 [3, 3, 64, 64], replicated, may hold values from -0.25 to 0.25
- entry_fraction: bfloat16 [2048, 128], P('tile'), may hold values from 0.019897461 to 0.19921875
- entry_target_tile: int32 [2048, 1], P('tile'), may hold values from 0 to 7; in each aligned block of 256 rows (0 to 255, 256 to 511, ...) at most 64 rows name the same one
- entry_owner_tile: int32 [2048], P('tile'), may hold values from 0 to 31
- entry_local_net: int32 [2048], P('tile'), may hold values from 0 to 63
- pin_demand_weight: float32 [2048], P('tile'), may hold values from 0.2 to 2
- pin_local_net: int32 [2048], P('tile'), may hold values from 0 to 63
- pin_global_cell: int32 [2048], P('tile'), may hold values from 0 to 511
Outputs:
- cell_grad: float32 [512], P('tile')
Inputs may be any that keep to these rules, and one draw needn't show every extreme that they name: `entry_target_tile`: among the entries of one tile index, at most 64 name the same destination, and in some tile index exactly 64 do.
All inputs are finite; a program needn't handle non-finite values.
Results may differ from a plain program's by a relative error of at most 0.0003.
Values may be sent and summed in bfloat16 or wider, within the bound.
A program may use at most 64 MiB of HBM per device.

v0:
```python
import jax
import jax.numpy as jnp
from jax import lax
from jax.sharding import PartitionSpec as P

NET_DEV = 64
CELL_DEV = 64
TILE_DEV = 32


def extended(array, sides, width):
    for axis, dim in sides:
        peers, length = (lax.axis_size(axis), array.shape[dim])
        up = [(i, (i + 1) % peers) for i in range(peers - 1)]
        down = [(j, i) for i, j in up]
        last = lax.slice_in_dim(array, length - width, length, axis=dim)
        leading = lax.slice_in_dim(array, 0, width, axis=dim)
        before = lax.ppermute(last, axis, up)
        after = lax.ppermute(leading, axis, down)
        array = jnp.concatenate([before, array, after], axis=dim)
    return array


def flipped_kernel(kernel):
    return jnp.transpose(kernel[::-1, ::-1], (0, 1, 3, 2))


def dilated_convolution(own_part, weights, channel_start, dilation):
    row_count, chan_own, col_count = own_part.shape
    rimmed = extended(own_part, (("tile", 0),), dilation)
    own_weights = lax.dynamic_slice_in_dim(weights, channel_start, chan_own, 3)
    start_sum = jnp.zeros((row_count, chan_own, col_count), jnp.float32)
    running = start_sum
    widened = jnp.pad(
        lax.all_gather(rimmed, "chan", axis=1, tiled=True), ((0, 0), (0, 0), (dilation, dilation))
    )
    for row_tap in range(3):
        for col_tap in range(3):
            part_in = widened[
                row_tap * dilation : row_tap * dilation + row_count,
                :,
                col_tap * dilation : col_tap * dilation + col_count,
            ]
            running = running + jnp.einsum(
                "rcw,co->row",
                part_in,
                own_weights[row_tap, col_tap],
                preferred_element_type=jnp.float32,
            )
    return running


def local(
    feat,
    lift,
    dilation4_weight,
    dilation8_weight,
    entry_fraction,
    entry_target_tile,
    entry_owner_tile,
    entry_local_net,
    pin_demand_weight,
    pin_local_net,
    pin_global_cell,
):
    highest = lax.Precision.HIGHEST
    tile_count = lax.axis_size("tile")
    chan_count = lax.axis_size("chan")
    row_count, chan_own, col_count = feat.shape
    channel_start = lax.axis_index("chan") * chan_own
    lift_own = lax.dynamic_slice_in_dim(lift, channel_start, chan_own, 0)
    entry_count = entry_target_tile.shape[0]
    capacity = chan_count * max(1, 2 * entry_count // (chan_count * tile_count))
    part_total = 1
    part_id = 0
    slot_count = capacity // part_total
    destination = entry_target_tile[:, 0]
    dest_hot = (destination[:, None] == jnp.arange(tile_count, dtype=jnp.int32)[None, :]).astype(
        jnp.int32
    )
    rank = jnp.sum(jnp.cumsum(dest_hot, axis=0) * dest_hot, axis=1) - 1
    placed = rank % part_total == part_id
    slot_row = jnp.where(
        placed, destination * slot_count + rank // part_total, tile_count * slot_count
    )
    pin_hot = (pin_local_net[None, :] == jnp.arange(NET_DEV, dtype=jnp.int32)[:, None]).astype(
        jnp.float32
    )
    strength = jnp.dot(pin_hot, pin_demand_weight, precision=highest)
    entry_hot = (entry_local_net[:, None] == jnp.arange(NET_DEV, dtype=jnp.int32)[None, :]).astype(
        jnp.float32
    )
    entry_strength = jnp.dot(entry_hot, strength, precision=highest)
    frac = entry_fraction.astype(jnp.float32)
    payload = entry_strength[:, None] * frac
    send_rows = (
        jnp.zeros((tile_count * slot_count, 128), jnp.float32)
        .at[slot_row]
        .set(payload, mode="drop")
    )
    send_ids = (
        jnp.zeros((tile_count * slot_count,), jnp.int32)
        .at[slot_row]
        .set(entry_owner_tile, mode="drop")
    )
    arrived, arrived_ids = (
        lax.all_to_all(
            send_rows.reshape(tile_count, slot_count, 128).astype(jnp.bfloat16),
            "tile",
            split_axis=0,
            concat_axis=0,
            tiled=True,
        ).astype(jnp.float32),
        lax.all_to_all(
            send_ids.reshape(tile_count, slot_count),
            "tile",
            split_axis=0,
            concat_axis=0,
            tiled=True,
        ),
    )
    tile_hot = (
        arrived_ids.reshape(-1)[:, None] == jnp.arange(TILE_DEV, dtype=jnp.int32)[None, :]
    ).astype(jnp.float32)
    tiles = jnp.dot(tile_hot.T, arrived.reshape(-1, 128), precision=highest)
    demand = (
        tiles.reshape(row_count // 8, col_count // 16, 8, 16)
        .transpose(0, 2, 1, 3)
        .reshape(row_count, col_count)
    )
    input_features = (
        feat.astype(jnp.float32) + demand[:, None, :] * lift_own[None, :, None]
    ).astype(jnp.bfloat16)
    first_preactivation = dilated_convolution(input_features, dilation4_weight, channel_start, 4)
    hidden_features = jax.nn.silu(first_preactivation).astype(jnp.bfloat16)
    second_output = dilated_convolution(hidden_features, dilation8_weight, channel_start, 8)
    second_gradient = jax.nn.sigmoid(second_output).astype(jnp.bfloat16)
    hidden_gradient = dilated_convolution(
        second_gradient, flipped_kernel(dilation8_weight), channel_start, 8
    )
    sigmoid_pre = jax.nn.sigmoid(first_preactivation)
    preactivation_gradient = (
        hidden_gradient * sigmoid_pre * (1.0 + first_preactivation * (1.0 - sigmoid_pre))
    ).astype(jnp.bfloat16)
    inputs_gradient = dilated_convolution(
        preactivation_gradient, flipped_kernel(dilation4_weight), channel_start, 4
    )
    partial_grad = jnp.sum(inputs_gradient * lift_own[None, :, None], axis=1)
    grad_demand = lax.psum(partial_grad, "chan")
    grad_tiles = (
        grad_demand.reshape(row_count // 8, 8, col_count // 16, 16)
        .transpose(0, 2, 1, 3)
        .reshape(TILE_DEV, 128)
    )
    slot_grads = jnp.dot(tile_hot, grad_tiles, precision=highest).reshape(
        tile_count, slot_count, 128
    )
    returned = lax.all_to_all(
        slot_grads.astype(jnp.bfloat16), "tile", split_axis=0, concat_axis=0, tiled=True
    ).astype(slot_grads.dtype)
    entry_rows = jnp.take(returned.reshape(-1, 128), slot_row, axis=0, mode="fill", fill_value=0.0)
    entry_grad = jnp.sum(entry_rows * frac, axis=1)
    grad_net = jnp.dot(entry_grad, entry_hot, precision=highest)
    pin_grad = jnp.dot(grad_net, pin_hot, precision=highest)
    cell_term = jax.ops.segment_sum(pin_grad, pin_global_cell, num_segments=CELL_DEV * tile_count)
    return lax.psum_scatter(cell_term, "tile", scatter_dimension=0, tiled=True)


def solution(mesh):
    in_specs = (
        P("tile", "chan", None),
        P(),
        P(),
        P(),
        P("tile", None),
        P("tile", None),
        P("tile"),
        P("tile"),
        P("tile"),
        P("tile"),
        P("tile"),
    )
    out_specs = P("tile")
    return jax.shard_map(local, mesh=mesh, in_specs=in_specs, out_specs=out_specs, check_vma=False)
```

profile of v0, /device:TPU:0, one launch (start us, length us, event | category | flops | bytes accessed | tf_op | source)
XLA Modules:
  0.0 194.8 jit_solution(14243430125302070767)
XLA Ops:
  9.6 1.6 scatter_custom_fusion
  11.8 7.3 %all-to-all-start = ((s32[8,1,64]{2,1,0:T(1,128)}), s32[8,1,64]{2,1,0:T(1,128)S(1)}, u32[]{:S(2)}, u32[]{:S(2)}) async-start(s32[8,1,64]{2,1,0:T(1,128)} %all_to_all.12), calls=%async_computation | async-start | bytes 8192 | tf_op jit(solution)/shard_map/all_to_all | solution.py:114
  19.9 0.9 fusion.42
  20.8 1.7 scatter_custom_fusion.1
  23.2 2.4 %all-to-all-done = s32[8,1,64]{2,1,0:T(1,128)S(1)} async-done(((s32[8,1,64]{2,1,0:T(1,128)}), s32[8,1,64]{2,1,0:T(1,128)S(1)}, u32[]{:S(2)}, u32[]{:S(2)}) %all-to-all-start) | async-done | bytes 2080 | tf_op jit(solution)/shard_map/all_to_all | solution.py:114
  25.6 3.6 %all-to-all-start.1 = ((bf16[8,64,128]{2,1,0:T(8,128)(2,1)}), bf16[8,64,128]{2,1,0:T(8,128)(2,1)S(1)}, u32[]{:S(2)}, u32[]{:S(2)}) async-start(bf16[8,64,128]{2,1,0:T(8,128)(2,1)} %bitcast.24), calls=%async_computation.1 | async-start | bytes 262144 | tf_op jit(solution)/shard_map/all_to_all | solution.py:107
  30.5 5.9 %all-to-all-done.1 = bf16[8,64,128]{2,1,0:T(8,128)(2,1)S(1)} async-done(((bf16[8,64,128]{2,1,0:T(8,128)(2,1)}), bf16[8,64,128]{2,1,0:T(8,128)(2,1)S(1)}, u32[]{:S(2)}, u32[]{:S(2)}) %all-to-all-start.1) | async-done | bytes 131104 | tf_op jit(solution)/shard_map/all_to_all | solution.py:107
  37.2 1.3 collective-permute-start.1
  38.5 4.5 %collective-permute-start = (bf16[4,16,256]{2,1,0:T(8,128)(2,1)S(1)}, bf16[4,16,256]{2,1,0:T(8,128)(2,1)S(1)}, u32[]{:S(2)}, u32[]{:S(2)}) collective-permute-start(bf16[4,16,256]{2,1,0:T(8,128)(2,1)S(1)} %get-tuple-element.13), channel_id=1, source_target_pairs={{0,4},{4,8},{8,12},{12,16},{16,20},{20,24},{24,28},{1,5},{5,9},{9,... | collective-permute-start | bytes 98312 | tf_op jit(solution)/shard_map/ppermute | solution.py:18
  43.1 1.6 collective-permute-done
  44.7 8.6 %all_gather.12 = bf16[24,64,256]{2,1,0:T(8,128)(2,1)S(1)} all-gather(bf16[24,16,256]{2,1,0:T(8,128)(2,1)S(1)} %pad_maximum_fusion.2), channel_id=1, replica_groups=mesh['tile'=8,'chan'=4] {'chan'}, dimensions={1}, use_global_device_ids=true | all-gather | bytes 983040 | tf_op jit(solution)/shard_map/all_gather | solution.py:35
  56.4 1.3 collective-permute-start.3
  57.7 4.9 %collective-permute-start.2 = (bf16[8,16,256]{2,1,0:T(8,128)(2,1)S(1)}, bf16[8,16,256]{2,1,0:T(8,128)(2,1)S(1)}, u32[]{:S(2)}, u32[]{:S(2)}) collective-permute-start(bf16[8,16,256]{2,1,0:T(8,128)(2,1)S(1)} %get-tuple-element.11), channel_id=1, source_target_pairs={{0,4},{4,8},{8,12},{12,16},{16,20},{20,24},{24,28},{1,5},{5,9},{9,... | collective-permute-start | bytes 196616 | tf_op jit(solution)/shard_map/ppermute | solution.py:18
  63.2 1.6 collective-permute-done.2
  65.6 17.1 %all-gather.3.cloned.1.call-done = bf16[32,64,256]{2,1,0:T(8,128)(2,1)} async-done(((bf16[32,16,256]{2,1,0:T(8,128)(2,1)}), bf16[32,64,256]{2,1,0:T(8,128)(2,1)}) %all-gather.3.cloned.1.call-update) | async-done | bytes 1048592 | tf_op jit(solution)/shard_map/all_gather | solution.py:35
  82.7 1.5 fusion.33
  86.9 1.6 fusion.46
  88.6 1.3 collective-permute-start.5
  89.9 4.7 %collective-permute-start.4 = (bf16[8,16,256]{2,0,1:T(8,128)(2,1)S(1)}, bf16[8,16,256]{2,0,1:T(8,128)(2,1)S(1)}, u32[]{:S(2)}, u32[]{:S(2)}) collective-permute-start(bf16[8,16,256]{2,0,1:T(8,128)(2,1)S(1)} %get-tuple-element.9), channel_id=1, source_target_pairs={{0,4},{4,8},{8,12},{12,16},{16,20},{20,24},{24,28},{1,5},{5,9},{9,... | collective-permute-start | bytes 196616 | tf_op jit(solution)/shard_map/ppermute | solution.py:18
  94.7 1.6 collective-permute-done.4
  97.2 18.6 %all-gather.5.cloned.1.call-done = bf16[32,64,256]{2,0,1:T(8,128)(2,1)} async-done(((bf16[32,16,256]{2,0,1:T(8,128)(2,1)}), bf16[32,64,256]{2,0,1:T(8,128)(2,1)}) %all-gather.5.cloned.1.call-update) | async-done | bytes 1048592 | tf_op jit(solution)/shard_map/all_gather | solution.py:35
  115.7 1.8 copy.66
  120.1 1.3 collective-permute-start.7
  121.4 4.5 %collective-permute-start.6 = (bf16[4,16,256]{2,1,0:T(8,128)(2,1)S(1)}, bf16[4,16,256]{2,1,0:T(8,128)(2,1)S(1)}, u32[]{:S(2)}, u32[]{:S(2)}) collective-permute-start(bf16[4,16,256]{2,1,0:T(8,128)(2,1)S(1)} %get-tuple-element.7), channel_id=1, source_target_pairs={{0,4},{4,8},{8,12},{12,16},{16,20},{20,24},{24,28},{1,5},{5,9},{9,... | collective-permute-start | bytes 98312 | tf_op jit(solution)/shard_map/ppermute | solution.py:18
  126.0 1.5 collective-permute-done.6
  127.6 7.5 %all_gather.15 = bf16[24,64,256]{2,1,0:T(8,128)(2,1)S(1)} all-gather(bf16[24,16,256]{2,1,0:T(8,128)(2,1)S(1)} %pad_maximum_fusion.3), channel_id=1, replica_groups=mesh['tile'=8,'chan'=4] {'chan'}, dimensions={1}, use_global_device_ids=true | all-gather | bytes 983040 | tf_op jit(solution)/shard_map/all_gather | solution.py:35
  137.8 11.7 %psum.7 = f32[32,128]{1,0:T(8,128)S(1)} all-reduce(f32[32,128]{1,0:T(8,128)S(1)} %reshape.105), channel_id=1, replica_groups=mesh['tile'=8,'chan'=4] {'chan'}, use_global_device_ids=true, to_apply=%region_6.7 | all-reduce | flops 4096 | bytes 32768 | tf_op jit(solution)/shard_map/psum | solution.py:149
  149.6 1.0 convolution_convert_fusion
  150.6 7.4 %all-to-all-start.2 = ((bf16[8,64,128]{2,1,0:T(8,128)(2,1)}), bf16[8,64,128]{2,1,0:T(8,128)(2,1)S(1)}, u32[]{:S(2)}, u32[]{:S(2)}) async-start(bf16[8,64,128]{2,1,0:T(8,128)(2,1)} %convolution_convert_fusion), calls=%async_computation.2 | async-start | bytes 262144 | tf_op jit(solution)/shard_map/all_to_all | solution.py:158
  159.3 6.1 %all-to-all-done.2 = bf16[8,64,128]{2,1,0:T(8,128)(2,1)S(1)} async-done(((bf16[8,64,128]{2,1,0:T(8,128)(2,1)}), bf16[8,64,128]{2,1,0:T(8,128)(2,1)S(1)}, u32[]{:S(2)}, u32[]{:S(2)}) %all-to-all-start.2) | async-done | bytes 131104 | tf_op jit(solution)/shard_map/all_to_all | solution.py:158
  166.7 2.5 %scatter_custom_fusion.2 = f32[512]{0:T(512)S(1)} fusion(s32[256]{0:T(256)} %param.21, f32[256]{0:T(256)S(1)} %bitcast.284, f32[]{:T(128)} %constant.62.clone.1), kind=kCustom, calls=%fused_computation.201 | custom fusion | flops 256 | bytes 2560 | tf_op jit(solution)/shard_map/scatter-add | solution.py:165
  169.2 18.2 %all-reduce.4 = f32[512]{0:T(512)S(1)} all-reduce(f32[512]{0:T(512)S(1)} %scatter_custom_fusion.2), channel_id=2, replica_groups=mesh['tile'=8,'chan'=4] {'tile'}, use_global_device_ids=true, to_apply=%region_9.10.clone | all-reduce | flops 512 | bytes 4096
  (106 shorter events, 23.3 us)
Async XLA Ops:
  6.5 12.6 %copy-start = (f32[256]{0:T(256)S(1)}, f32[256]{0:T(256)}, u32[]{:S(2)}) copy-start(f32[256]{0:T(256)} %param.19) | copy-start | bytes 3076
  6.5 22.7 %copy-start.8 = (f32[64]{0:T(128)S(1)}, f32[64]{0:T(128)}, u32[]{:S(2)}) copy-start(f32[64]{0:T(128)} %param.12) | copy-start | bytes 772
  6.5 30.5 %copy-start.5 = (bf16[16,16,256]{2,1,0:T(8,128)(2,1)S(1)}, bf16[16,16,256]{2,1,0:T(8,128)(2,1)}, u32[]{:S(2)}) copy-start(bf16[16,16,256]{2,1,0:T(8,128)(2,1)} %param.11) | copy-start | bytes 393220
  11.8 13.8 %all-to-all-start = ((s32[8,1,64]{2,1,0:T(1,128)}), s32[8,1,64]{2,1,0:T(1,128)S(1)}, u32[]{:S(2)}, u32[]{:S(2)}) async-start(s32[8,1,64]{2,1,0:T(1,128)} %all_to_all.12), calls=%async_computation | async-start | bytes 8192 | tf_op jit(solution)/shard_map/all_to_all | solution.py:114
  25.6 10.9 %all-to-all-start.1 = ((bf16[8,64,128]{2,1,0:T(8,128)(2,1)}), bf16[8,64,128]{2,1,0:T(8,128)(2,1)S(1)}, u32[]{:S(2)}, u32[]{:S(2)}) async-start(bf16[8,64,128]{2,1,0:T(8,128)(2,1)} %bitcast.24), calls=%async_computation.1 | async-start | bytes 262144 | tf_op jit(solution)/shard_map/all_to_all | solution.py:107
  29.2 53.6 %all-gather.3.cloned.1.call-start = ((), (), s32[]{:S(2)}) async-start(), calls=%async_computation.3 | async-start | bytes 1310720 | tf_op jit(solution)/shard_map/all_gather | solution.py:35
  36.6 16.7 %copy-start.3 = (bf16[3,3,64,64]{3,2,1,0:T(8,128)(2,1)S(1)}, bf16[3,3,64,64]{3,2,1,0:T(8,128)(2,1)}, u32[]{:S(2)}) copy-start(bf16[3,3,64,64]{3,2,1,0:T(8,128)(2,1)} %param.13) | copy-start | bytes 221188
  37.2 5.9 %collective-permute-start.1 = (bf16[4,16,256]{2,1,0:T(8,128)(2,1)S(1)}, bf16[4,16,256]{2,1,0:T(8,128)(2,1)S(1)}, u32[]{:S(2)}, u32[]{:S(2)}) collective-permute-start(bf16[4,16,256]{2,1,0:T(8,128)(2,1)S(1)} %get-tuple-element.14), channel_id=1, source_target_pairs={{4,0},{8,4},{12,8},{16,12},{20,16},{24,20},{28,24},{5,1},{9,5},{13... | collective-permute-start | bytes 98312 | tf_op jit(solution)/shard_map/ppermute | solution.py:19
  38.5 6.1 %collective-permute-start = (bf16[4,16,256]{2,1,0:T(8,128)(2,1)S(1)}, bf16[4,16,256]{2,1,0:T(8,128)(2,1)S(1)}, u32[]{:S(2)}, u32[]{:S(2)}) collective-permute-start(bf16[4,16,256]{2,1,0:T(8,128)(2,1)S(1)} %get-tuple-element.13), channel_id=1, source_target_pairs={{0,4},{4,8},{8,12},{12,16},{16,20},{20,24},{24,28},{1,5},{5,9},{9,... | collective-permute-start | bytes 98312 | tf_op jit(solution)/shard_map/ppermute | solution.py:18
  56.0 26.7 %copy-start.2 = (bf16[3,3,64,64]{3,2,1,0:T(8,128)(2,1)S(1)}, bf16[3,3,64,64]{3,2,1,0:T(8,128)(2,1)}, u32[]{:S(2)}) copy-start(bf16[3,3,64,64]{3,2,1,0:T(8,128)(2,1)} %param.14) | copy-start | bytes 221188
  56.4 6.8 %collective-permute-start.3 = (bf16[8,16,256]{2,1,0:T(8,128)(2,1)S(1)}, bf16[8,16,256]{2,1,0:T(8,128)(2,1)S(1)}, u32[]{:S(2)}, u32[]{:S(2)}) collective-permute-start(bf16[8,16,256]{2,1,0:T(8,128)(2,1)S(1)} %get-tuple-element.12), channel_id=1, source_target_pairs={{4,0},{8,4},{12,8},{16,12},{20,16},{24,20},{28,24},{5,1},{9,5},{13... | collective-permute-start | bytes 196616 | tf_op jit(solution)/shard_map/ppermute | solution.py:19
  57.7 7.1 %collective-permute-start.2 = (bf16[8,16,256]{2,1,0:T(8,128)(2,1)S(1)}, bf16[8,16,256]{2,1,0:T(8,128)(2,1)S(1)}, u32[]{:S(2)}, u32[]{:S(2)}) collective-permute-start(bf16[8,16,256]{2,1,0:T(8,128)(2,1)S(1)} %get-tuple-element.11), channel_id=1, source_target_pairs={{0,4},{4,8},{8,12},{12,16},{16,20},{20,24},{24,28},{1,5},{5,9},{9,... | collective-permute-start | bytes 196616 | tf_op jit(solution)/shard_map/ppermute | solution.py:18
  65.6 50.2 %all-gather.5.cloned.1.call-start = ((), (), s32[]{:S(2)}) async-start(), calls=%async_computation.4 | async-start | bytes 1310720 | tf_op jit(solution)/shard_map/all_gather | solution.py:35
  82.7 1.5 copy-start.1
  88.6 6.2 %collective-permute-start.5 = (bf16[8,16,256]{2,0,1:T(8,128)(2,1)S(1)}, bf16[8,16,256]{2,0,1:T(8,128)(2,1)S(1)}, u32[]{:S(2)}, u32[]{:S(2)}) collective-permute-start(bf16[8,16,256]{2,0,1:T(8,128)(2,1)S(1)} %get-tuple-element.10), channel_id=1, source_target_pairs={{4,0},{8,4},{12,8},{16,12},{20,16},{24,20},{28,24},{5,1},{9,5},{13... | collective-permute-start | bytes 196616 | tf_op jit(solution)/shard_map/ppermute | solution.py:19
  89.9 6.4 %collective-permute-start.4 = (bf16[8,16,256]{2,0,1:T(8,128)(2,1)S(1)}, bf16[8,16,256]{2,0,1:T(8,128)(2,1)S(1)}, u32[]{:S(2)}, u32[]{:S(2)}) collective-permute-start(bf16[8,16,256]{2,0,1:T(8,128)(2,1)S(1)} %get-tuple-element.9), channel_id=1, source_target_pairs={{0,4},{4,8},{8,12},{12,16},{16,20},{20,24},{24,28},{1,5},{5,9},{9,... | collective-permute-start | bytes 196616 | tf_op jit(solution)/shard_map/ppermute | solution.py:18
  120.1 5.9 %collective-permute-start.7 = (bf16[4,16,256]{2,1,0:T(8,128)(2,1)S(1)}, bf16[4,16,256]{2,1,0:T(8,128)(2,1)S(1)}, u32[]{:S(2)}, u32[]{:S(2)}) collective-permute-start(bf16[4,16,256]{2,1,0:T(8,128)(2,1)S(1)} %get-tuple-element.8), channel_id=1, source_target_pairs={{4,0},{8,4},{12,8},{16,12},{20,16},{24,20},{28,24},{5,1},{9,5},{13... | collective-permute-start | bytes 98312 | tf_op jit(solution)/shard_map/ppermute | solution.py:19
  121.4 6.1 %collective-permute-start.6 = (bf16[4,16,256]{2,1,0:T(8,128)(2,1)S(1)}, bf16[4,16,256]{2,1,0:T(8,128)(2,1)S(1)}, u32[]{:S(2)}, u32[]{:S(2)}) collective-permute-start(bf16[4,16,256]{2,1,0:T(8,128)(2,1)S(1)} %get-tuple-element.7), channel_id=1, source_target_pairs={{0,4},{4,8},{8,12},{12,16},{16,20},{20,24},{24,28},{1,5},{5,9},{9,... | collective-permute-start | bytes 98312 | tf_op jit(solution)/shard_map/ppermute | solution.py:18
  137.2 20.8 %copy-start.9 = (u32[32]{0:T(128)S(1)}, u32[32]{0:T(128)}, u32[]{:S(2)}) copy-start(u32[32]{0:T(128)} %constant.82) | copy-start | bytes 388
  137.8 28.3 %copy-start.4 = (bf16[256,128]{1,0:T(8,128)(2,1)S(1)}, bf16[256,128]{1,0:T(8,128)(2,1)}, u32[]{:S(2)}) copy-start(bf16[256,128]{1,0:T(8,128)(2,1)} %param.15) | copy-start | bytes 196612
  150.6 15.7 %copy-start.6 = (s32[256]{0:T(256)S(1)}, s32[256]{0:T(256)}, u32[]{:S(2)}) copy-start(s32[256]{0:T(256)} %param.18) | copy-start | bytes 3076
  150.6 15.9 %copy-start.7 = (s32[256]{0:T(256)S(1)}, s32[256]{0:T(256)}, u32[]{:S(2)}) copy-start(s32[256]{0:T(256)} %param.20) | copy-start | bytes 3076
  150.6 14.7 %all-to-all-start.2 = ((bf16[8,64,128]{2,1,0:T(8,128)(2,1)}), bf16[8,64,128]{2,1,0:T(8,128)(2,1)S(1)}, u32[]{:S(2)}, u32[]{:S(2)}) async-start(bf16[8,64,128]{2,1,0:T(8,128)(2,1)} %convolution_convert_fusion), calls=%async_computation.2 | async-start | bytes 262144 | tf_op jit(solution)/shard_map/all_to_all | solution.py:158
Sparse Core Ops, SparseCore 0:
  65.7 16.9 all-gather.2
  97.2 18.4 all-gather.4
where the time goes:
time: 196 us; the launch traced here: 195 us
  waiting for transfers between devices  57.2 us (29%)
  blocking collectives  46 us (23%)
  starting transfers between devices  42.2 us (22%)
  matrix products  15.8 us (8%)
  between operations  14.4 us (7%)
  other arithmetic  11.8 us (6%)
  local copies, waits for them, and re-layouts  7.41 us (4%)
    all_gather x2, waiting for transfers between devices, dilated_convolution(): lax.all_gather(rimmed, 'chan', axis=1, tiled=True)  35.7 us
    ppermute x4, starting transfers between devices, extended(): before = lax.ppermute(last, axis, up)  18.7 us
    unnamed x1, blocking collectives  18.2 us
    all_gather x2, blocking collectives, dilated_convolution(): lax.all_gather(rimmed, 'chan', axis=1, tiled=True)  16.1 us
    dot_general x36, matrix products, dilated_convolution(): jnp.einsum('rcw,co->row', part_in, own_weights[row_tap, col_tap], preferr...  12.4 us
    psum x1, blocking collectives, local(): grad_demand = lax.psum(partial_grad, 'chan')  11.7 us
    all_to_all x1, starting transfers between devices, local(): lax.all_to_all(slot_grads.astype(jnp.bfloat16), 'tile', split_axis=0, con...  7.38 us
    all_to_all x1, starting transfers between devices, local(): lax.all_to_all(send_ids.reshape(tile_count, slot_count), 'tile', split_ax...  7.31 us
  transfers between devices with their start and end apart: 13, of which 11 were waited for; matrix products, arithmetic and copies ran while one was open for 3% of the time, Pallas kernels for 0%

commit v1 on v0

--- a/solution.py
+++ b/solution.py
@@ -32,7 +32,8 @@
     start_sum = jnp.zeros((row_count, chan_own, col_count), jnp.float32)
     running = start_sum
     widened = jnp.pad(
-        lax.all_gather(rimmed, "chan", axis=1, tiled=True), ((0, 0), (0, 0), (dilation, dilation))
+        jnp.concatenate(lax.all_gather(rimmed, "chan"), axis=1),
+        ((0, 0), (0, 0), (dilation, dilation)),
     )
     for row_tap in range(3):
         for col_tap in range(3):

time: 196 us -> 198 us (1.010)
  starting transfers between devices: 42.2 us -> 34.7 us
  waiting for transfers between devices: 57.2 us -> 64.2 us
  local copies, waits for them, and re-layouts: 7.41 us -> 11.5 us
    ppermute x4, waiting for transfers between devices: 0.79 us -> 17 us  [extended(): after = lax.ppermute(leading, axis, down)]
    ppermute x4, starting transfers between devices: 18.7 us -> 12.8 us  [extended(): before = lax.ppermute(last, axis, up)]
    ppermute x4, waiting for transfers between devices: 6.25 us -> 1.52 us  [extended(): before = lax.ppermute(last, axis, up)]
    all_gather x2, waiting for transfers between devices: 35.7 us -> 31.1 us  [dilated_convolution(): lax.all_gather(rimmed, 'chan')]
    slice x1 -> x8, local copies, waits for them, and re-layouts: 0.21 us -> 3.22 us  [the longest x7 3 us: dilated_convolution(): widened[row_tap * dilation:row_tap * dilation + row_count, :, col_tap * d...]
  transfers between devices with their start and end apart: 13 -> 13, of which waited for: 11 -> 13; matrix products, arithmetic and copies ran while one was open for 3% -> 3% of each run, Pallas kernels for 0% -> 0%
where the time goes in v1:
time: 198 us; the launch traced here: 197 us
  waiting for transfers between devices  64.2 us (32%)
  blocking collectives  46 us (23%)
  starting transfers between devices  34.7 us (18%)
  matrix products  14.7 us (7%)
  between operations  14.5 us (7%)
  other arithmetic  11.7 us (6%)
  local copies, waits for them, and re-layouts  11.5 us (6%)
    all_gather x2, waiting for transfers between devices, dilated_convolution(): lax.all_gather(rimmed, 'chan')  31.1 us
    unnamed x1, blocking collectives  18.2 us
    ppermute x4, waiting for transfers between devices, extended(): after = lax.ppermute(leading, axis, down)  17 us
    all_gather x2, blocking collectives, dilated_convolution(): lax.all_gather(rimmed, 'chan')  16.3 us
    ppermute x4, starting transfers between devices, extended(): before = lax.ppermute(last, axis, up)  12.8 us
    psum x1, blocking collectives, local(): grad_demand = lax.psum(partial_grad, 'chan')  11.5 us
    dot_general x36, matrix products, dilated_convolution(): jnp.einsum('rcw,co->row', part_in, own_weights[row_tap, col_tap], preferr...  11.2 us
    all_to_all x1, starting transfers between devices, local(): lax.all_to_all(send_ids.reshape(tile_count, slot_count), 'tile', split_ax...  7.31 us
  transfers between devices with their start and end apart: 13, of which 13 were waited for; matrix products, arithmetic and copies ran while one was open for 3% of the time, Pallas kernels for 0%

profile of v1, /device:TPU:0, one launch (start us, length us, event | category | flops | bytes accessed | tf_op | source)
XLA Modules:
  0.0 197.3 jit_solution(3670143812291627563)
XLA Ops:
  9.6 1.6 scatter_custom_fusion
  11.8 7.3 %all-to-all-start = ((s32[8,1,64]{2,1,0:T(1,128)}), s32[8,1,64]{2,1,0:T(1,128)S(1)}, u32[]{:S(2)}, u32[]{:S(2)}) async-start(s32[8,1,64]{2,1,0:T(1,128)} %all_to_all.12), calls=%async_computation | async-start | bytes 8192 | tf_op jit(solution)/shard_map/all_to_all | solution.py:115
  19.9 0.9 fusion.23
  20.8 1.7 scatter_custom_fusion.1
  23.2 2.4 %all-to-all-done = s32[8,1,64]{2,1,0:T(1,128)S(1)} async-done(((s32[8,1,64]{2,1,0:T(1,128)}), s32[8,1,64]{2,1,0:T(1,128)S(1)}, u32[]{:S(2)}, u32[]{:S(2)}) %all-to-all-start) | async-done | bytes 2080 | tf_op jit(solution)/shard_map/all_to_all | solution.py:115
  25.6 3.6 %all-to-all-start.1 = ((bf16[8,64,128]{2,1,0:T(8,128)(2,1)}), bf16[8,64,128]{2,1,0:T(8,128)(2,1)S(1)}, u32[]{:S(2)}, u32[]{:S(2)}) async-start(bf16[8,64,128]{2,1,0:T(8,128)(2,1)} %bitcast.24), calls=%async_computation.1 | async-start | bytes 262144 | tf_op jit(solution)/shard_map/all_to_all | solution.py:108
  30.6 5.9 %all-to-all-done.1 = bf16[8,64,128]{2,1,0:T(8,128)(2,1)S(1)} async-done(((bf16[8,64,128]{2,1,0:T(8,128)(2,1)}), bf16[8,64,128]{2,1,0:T(8,128)(2,1)S(1)}, u32[]{:S(2)}, u32[]{:S(2)}) %all-to-all-start.1) | async-done | bytes 131104 | tf_op jit(solution)/shard_map/all_to_all | solution.py:108
  37.2 2.1 %collective-permute-start = (bf16[4,16,256]{2,1,0:T(8,128)(2,1)S(1)}, bf16[4,16,256]{2,1,0:T(8,128)(2,1)S(1)}, u32[]{:S(2)}, u32[]{:S(2)}) collective-permute-start(bf16[4,16,256]{2,1,0:T(8,128)(2,1)S(1)} %get-tuple-element.31), channel_id=1, source_target_pairs={{0,4},{4,8},{8,12},{12,16},{16,20},{20,24},{24,28},{1,5},{5,9},{9,... | collective-permute-start | bytes 98312 | tf_op jit(solution)/shard_map/ppermute | solution.py:18
  39.3 1.3 collective-permute-start.1
  40.9 4.2 %collective-permute-done.1 = bf16[4,16,256]{2,1,0:T(8,128)(2,1)S(1)} collective-permute-done((bf16[4,16,256]{2,1,0:T(8,128)(2,1)S(1)}, bf16[4,16,256]{2,1,0:T(8,128)(2,1)S(1)}, u32[]{:S(2)}, u32[]{:S(2)}) %collective-permute-start.1) | collective-permute-done | bytes 32800 | tf_op jit(solution)/shard_map/ppermute | solution.py:19
  45.2 8.6 %all-gather = bf16[96,16,256]{2,1,0:T(8,128)(2,1)S(1)} all-gather(bf16[24,16,256]{2,1,0:T(8,128)(2,1)S(1)} %pad_maximum_fusion.2), channel_id=2, replica_groups=mesh['tile'=8,'chan'=4] {'chan'}, dimensions={0}, use_global_device_ids=true | all-gather | bytes 983040 | tf_op jit(solution)/shard_map/all_gather | solution.py:35
  57.9 3.9 %collective-permute-start.2 = (bf16[8,16,256]{2,1,0:T(8,128)(2,1)S(1)}, bf16[8,16,256]{2,1,0:T(8,128)(2,1)S(1)}, u32[]{:S(2)}, u32[]{:S(2)}) collective-permute-start(bf16[8,16,256]{2,1,0:T(8,128)(2,1)S(1)} %get-tuple-element.29), channel_id=1, source_target_pairs={{0,4},{4,8},{8,12},{12,16},{16,20},{20,24},{24,28},{1,5},{5,9},{9,... | collective-permute-start | bytes 196616 | tf_op jit(solution)/shard_map/ppermute | solution.py:18
  61.8 1.3 collective-permute-start.3
  63.7 4.3 %collective-permute-done.3 = bf16[8,16,256]{2,1,0:T(8,128)(2,1)S(1)} collective-permute-done((bf16[8,16,256]{2,1,0:T(8,128)(2,1)S(1)}, bf16[8,16,256]{2,1,0:T(8,128)(2,1)S(1)}, u32[]{:S(2)}, u32[]{:S(2)}) %collective-permute-start.3) | collective-permute-done | bytes 65568 | tf_op jit(solution)/shard_map/ppermute | solution.py:19
  68.8 14.4 %all-gather.7.cloned.1.call-done = bf16[128,16,256]{2,1,0:T(8,128)(2,1)} async-done(((bf16[32,16,256]{2,1,0:T(8,128)(2,1)}), bf16[128,16,256]{2,1,0:T(8,128)(2,1)}) %all-gather.7.cloned.1.call-update) | async-done | bytes 1048592 | tf_op jit(solution)/shard_map/all_gather | solution.py:35
  83.1 1.4 copy.178
  87.8 1.6 fusion.27
  89.4 3.4 %collective-permute-start.4 = (bf16[8,16,256]{2,0,1:T(8,128)(2,1)S(1)}, bf16[8,16,256]{2,0,1:T(8,128)(2,1)S(1)}, u32[]{:S(2)}, u32[]{:S(2)}) collective-permute-start(bf16[8,16,256]{2,0,1:T(8,128)(2,1)S(1)} %get-tuple-element.27), channel_id=1, source_target_pairs={{0,4},{4,8},{8,12},{12,16},{16,20},{20,24},{24,28},{1,5},{5,9},{9,... | collective-permute-start | bytes 196616 | tf_op jit(solution)/shard_map/ppermute | solution.py:18
  92.8 1.5 collective-permute-start.5
  94.7 4.3 %collective-permute-done.5 = bf16[8,16,256]{2,0,1:T(8,128)(2,1)S(1)} collective-permute-done((bf16[8,16,256]{2,0,1:T(8,128)(2,1)S(1)}, bf16[8,16,256]{2,0,1:T(8,128)(2,1)S(1)}, u32[]{:S(2)}, u32[]{:S(2)}) %collective-permute-start.5) | collective-permute-done | bytes 65568 | tf_op jit(solution)/shard_map/ppermute | solution.py:19
  99.8 16.8 %all-gather.9.cloned.1.call-done = bf16[128,16,256]{2,0,1:T(8,128)(2,1)} async-done(((bf16[32,16,256]{2,0,1:T(8,128)(2,1)}), bf16[128,16,256]{2,0,1:T(8,128)(2,1)}) %all-gather.9.cloned.1.call-update) | async-done | bytes 1048592 | tf_op jit(solution)/shard_map/all_gather | solution.py:35
  116.6 1.6 fusion.91
  122.3 3.4 %collective-permute-start.6 = (bf16[4,16,256]{2,1,0:T(8,128)(2,1)S(1)}, bf16[4,16,256]{2,1,0:T(8,128)(2,1)S(1)}, u32[]{:S(2)}, u32[]{:S(2)}) collective-permute-start(bf16[4,16,256]{2,1,0:T(8,128)(2,1)S(1)} %get-tuple-element.25), channel_id=1, source_target_pairs={{0,4},{4,8},{8,12},{12,16},{16,20},{20,24},{24,28},{1,5},{5,9},{9,... | collective-permute-start | bytes 98312 | tf_op jit(solution)/shard_map/ppermute | solution.py:18
  125.7 1.3 collective-permute-start.7
  127.3 4.2 %collective-permute-done.7 = bf16[4,16,256]{2,1,0:T(8,128)(2,1)S(1)} collective-permute-done((bf16[4,16,256]{2,1,0:T(8,128)(2,1)S(1)}, bf16[4,16,256]{2,1,0:T(8,128)(2,1)S(1)}, u32[]{:S(2)}, u32[]{:S(2)}) %collective-permute-start.7) | collective-permute-done | bytes 32800 | tf_op jit(solution)/shard_map/ppermute | solution.py:19
  131.6 7.7 %all-gather.3 = bf16[96,16,256]{2,1,0:T(8,128)(2,1)S(1)} all-gather(bf16[24,16,256]{2,1,0:T(8,128)(2,1)S(1)} %pad_maximum_fusion.3), channel_id=5, replica_groups=mesh['tile'=8,'chan'=4] {'chan'}, dimensions={0}, use_global_device_ids=true | all-gather | bytes 983040 | tf_op jit(solution)/shard_map/all_gather | solution.py:35
  142.3 11.5 %psum.7 = f32[32,128]{1,0:T(8,128)S(1)} all-reduce(f32[32,128]{1,0:T(8,128)S(1)} %reshape.149), channel_id=1, replica_groups=mesh['tile'=8,'chan'=4] {'chan'}, use_global_device_ids=true, to_apply=%region_6.7 | all-reduce | flops 4096 | bytes 32768 | tf_op jit(solution)/shard_map/psum | solution.py:150
  153.9 1.1 convolution_convert_fusion
  154.9 5.6 %all-to-all-start.2 = ((bf16[8,64,128]{2,1,0:T(8,128)(2,1)}), bf16[8,64,128]{2,1,0:T(8,128)(2,1)S(1)}, u32[]{:S(2)}, u32[]{:S(2)}) async-start(bf16[8,64,128]{2,1,0:T(8,128)(2,1)} %convolution_convert_fusion), calls=%async_computation.2 | async-start | bytes 262144 | tf_op jit(solution)/shard_map/all_to_all | solution.py:159
  161.8 6.1 %all-to-all-done.2 = bf16[8,64,128]{2,1,0:T(8,128)(2,1)S(1)} async-done(((bf16[8,64,128]{2,1,0:T(8,128)(2,1)}), bf16[8,64,128]{2,1,0:T(8,128)(2,1)S(1)}, u32[]{:S(2)}, u32[]{:S(2)}) %all-to-all-start.2) | async-done | bytes 131104 | tf_op jit(solution)/shard_map/all_to_all | solution.py:159
  169.2 2.5 %scatter_custom_fusion.2 = f32[512]{0:T(512)S(1)} fusion(s32[256]{0:T(256)} %param.21, f32[256]{0:T(256)S(1)} %bitcast.374, f32[]{:T(128)} %constant.62.clone.1), kind=kCustom, calls=%fused_computation.187 | custom fusion | flops 256 | bytes 2560 | tf_op jit(solution)/shard_map/scatter-add | solution.py:166
  171.7 18.2 %all-reduce.4 = f32[512]{0:T(512)S(1)} all-reduce(f32[512]{0:T(512)S(1)} %scatter_custom_fusion.2), channel_id=6, replica_groups=mesh['tile'=8,'chan'=4] {'tile'}, use_global_device_ids=true, to_apply=%region_9.10.clone | all-reduce | flops 512 | bytes 4096
  (116 shorter events, 27.4 us)
Async XLA Ops:
  6.5 12.6 %copy-start = (f32[256]{0:T(256)S(1)}, f32[256]{0:T(256)}, u32[]{:S(2)}) copy-start(f32[256]{0:T(256)} %param.19) | copy-start | bytes 3076
  6.5 22.7 %copy-start.8 = (f32[64]{0:T(128)S(1)}, f32[64]{0:T(128)}, u32[]{:S(2)}) copy-start(f32[64]{0:T(128)} %param.12) | copy-start | bytes 772
  6.5 30.5 %copy-start.5 = (bf16[16,16,256]{2,1,0:T(8,128)(2,1)S(1)}, bf16[16,16,256]{2,1,0:T(8,128)(2,1)}, u32[]{:S(2)}) copy-start(bf16[16,16,256]{2,1,0:T(8,128)(2,1)} %param.11) | copy-start | bytes 393220
  11.8 13.8 %all-to-all-start = ((s32[8,1,64]{2,1,0:T(1,128)}), s32[8,1,64]{2,1,0:T(1,128)S(1)}, u32[]{:S(2)}, u32[]{:S(2)}) async-start(s32[8,1,64]{2,1,0:T(1,128)} %all_to_all.12), calls=%async_computation | async-start | bytes 8192 | tf_op jit(solution)/shard_map/all_to_all | solution.py:115
  25.6 10.9 %all-to-all-start.1 = ((bf16[8,64,128]{2,1,0:T(8,128)(2,1)}), bf16[8,64,128]{2,1,0:T(8,128)(2,1)S(1)}, u32[]{:S(2)}, u32[]{:S(2)}) async-start(bf16[8,64,128]{2,1,0:T(8,128)(2,1)} %bitcast.24), calls=%async_computation.1 | async-start | bytes 262144 | tf_op jit(solution)/shard_map/all_to_all | solution.py:108
  29.2 54.0 %all-gather.7.cloned.1.call-start = ((), (), s32[]{:S(2)}) async-start(), calls=%async_computation.3 | async-start | bytes 1310720 | tf_op jit(solution)/shard_map/all_gather | solution.py:35
  37.2 3.7 %collective-permute-start = (bf16[4,16,256]{2,1,0:T(8,128)(2,1)S(1)}, bf16[4,16,256]{2,1,0:T(8,128)(2,1)S(1)}, u32[]{:S(2)}, u32[]{:S(2)}) collective-permute-start(bf16[4,16,256]{2,1,0:T(8,128)(2,1)S(1)} %get-tuple-element.31), channel_id=1, source_target_pairs={{0,4},{4,8},{8,12},{12,16},{16,20},{20,24},{24,28},{1,5},{5,9},{9,... | collective-permute-start | bytes 98312 | tf_op jit(solution)/shard_map/ppermute | solution.py:18
  39.3 5.8 %collective-permute-start.1 = (bf16[4,16,256]{2,1,0:T(8,128)(2,1)S(1)}, bf16[4,16,256]{2,1,0:T(8,128)(2,1)S(1)}, u32[]{:S(2)}, u32[]{:S(2)}) collective-permute-start(bf16[4,16,256]{2,1,0:T(8,128)(2,1)S(1)} %get-tuple-element.32), channel_id=1, source_target_pairs={{4,0},{8,4},{12,8},{16,12},{20,16},{24,20},{28,24},{5,1},{9,5},{13... | collective-permute-start | bytes 98312 | tf_op jit(solution)/shard_map/ppermute | solution.py:19
  53.8 0.9 copy-start.3
  57.9 5.8 %collective-permute-start.2 = (bf16[8,16,256]{2,1,0:T(8,128)(2,1)S(1)}, bf16[8,16,256]{2,1,0:T(8,128)(2,1)S(1)}, u32[]{:S(2)}, u32[]{:S(2)}) collective-permute-start(bf16[8,16,256]{2,1,0:T(8,128)(2,1)S(1)} %get-tuple-element.29), channel_id=1, source_target_pairs={{0,4},{4,8},{8,12},{12,16},{16,20},{20,24},{24,28},{1,5},{5,9},{9,... | collective-permute-start | bytes 196616 | tf_op jit(solution)/shard_map/ppermute | solution.py:18
  61.8 6.2 %collective-permute-start.3 = (bf16[8,16,256]{2,1,0:T(8,128)(2,1)S(1)}, bf16[8,16,256]{2,1,0:T(8,128)(2,1)S(1)}, u32[]{:S(2)}, u32[]{:S(2)}) collective-permute-start(bf16[8,16,256]{2,1,0:T(8,128)(2,1)S(1)} %get-tuple-element.30), channel_id=1, source_target_pairs={{4,0},{8,4},{12,8},{16,12},{20,16},{24,20},{28,24},{5,1},{9,5},{13... | collective-permute-start | bytes 196616 | tf_op jit(solution)/shard_map/ppermute | solution.py:19
  68.7 47.9 %all-gather.9.cloned.1.call-start = ((), (), s32[]{:S(2)}) async-start(), calls=%async_computation.4 | async-start | bytes 1310720 | tf_op jit(solution)/shard_map/all_gather | solution.py:35
  83.1 1.4 copy-start.2
  89.4 5.3 %collective-permute-start.4 = (bf16[8,16,256]{2,0,1:T(8,128)(2,1)S(1)}, bf16[8,16,256]{2,0,1:T(8,128)(2,1)S(1)}, u32[]{:S(2)}, u32[]{:S(2)}) collective-permute-start(bf16[8,16,256]{2,0,1:T(8,128)(2,1)S(1)} %get-tuple-element.27), channel_id=1, source_target_pairs={{0,4},{4,8},{8,12},{12,16},{16,20},{20,24},{24,28},{1,5},{5,9},{9,... | collective-permute-start | bytes 196616 | tf_op jit(solution)/shard_map/ppermute | solution.py:18
  92.8 6.2 %collective-permute-start.5 = (bf16[8,16,256]{2,0,1:T(8,128)(2,1)S(1)}, bf16[8,16,256]{2,0,1:T(8,128)(2,1)S(1)}, u32[]{:S(2)}, u32[]{:S(2)}) collective-permute-start(bf16[8,16,256]{2,0,1:T(8,128)(2,1)S(1)} %get-tuple-element.28), channel_id=1, source_target_pairs={{4,0},{8,4},{12,8},{16,12},{20,16},{24,20},{28,24},{5,1},{9,5},{13... | collective-permute-start | bytes 196616 | tf_op jit(solution)/shard_map/ppermute | solution.py:19
  116.6 1.7 copy-start.1
  122.3 5.0 %collective-permute-start.6 = (bf16[4,16,256]{2,1,0:T(8,128)(2,1)S(1)}, bf16[4,16,256]{2,1,0:T(8,128)(2,1)S(1)}, u32[]{:S(2)}, u32[]{:S(2)}) collective-permute-start(bf16[4,16,256]{2,1,0:T(8,128)(2,1)S(1)} %get-tuple-element.25), channel_id=1, source_target_pairs={{0,4},{4,8},{8,12},{12,16},{16,20},{20,24},{24,28},{1,5},{5,9},{9,... | collective-permute-start | bytes 98312 | tf_op jit(solution)/shard_map/ppermute | solution.py:18
  125.7 5.8 %collective-permute-start.7 = (bf16[4,16,256]{2,1,0:T(8,128)(2,1)S(1)}, bf16[4,16,256]{2,1,0:T(8,128)(2,1)S(1)}, u32[]{:S(2)}, u32[]{:S(2)}) collective-permute-start(bf16[4,16,256]{2,1,0:T(8,128)(2,1)S(1)} %get-tuple-element.26), channel_id=1, source_target_pairs={{4,0},{8,4},{12,8},{16,12},{20,16},{24,20},{28,24},{5,1},{9,5},{13... | collective-permute-start | bytes 98312 | tf_op jit(solution)/shard_map/ppermute | solution.py:19
  141.7 18.8 %copy-start.9 = (u32[32]{0:T(128)S(1)}, u32[32]{0:T(128)}, u32[]{:S(2)}) copy-start(u32[32]{0:T(128)} %constant.82) | copy-start | bytes 388
  142.3 26.3 %copy-start.4 = (bf16[256,128]{1,0:T(8,128)(2,1)S(1)}, bf16[256,128]{1,0:T(8,128)(2,1)}, u32[]{:S(2)}) copy-start(bf16[256,128]{1,0:T(8,128)(2,1)} %param.15) | copy-start | bytes 196612
  154.9 13.9 %copy-start.6 = (s32[256]{0:T(256)S(1)}, s32[256]{0:T(256)}, u32[]{:S(2)}) copy-start(s32[256]{0:T(256)} %param.18) | copy-start | bytes 3076
  154.9 14.2 %copy-start.7 = (s32[256]{0:T(256)S(1)}, s32[256]{0:T(256)}, u32[]{:S(2)}) copy-start(s32[256]{0:T(256)} %param.20) | copy-start | bytes 3076
  154.9 13.0 %all-to-all-start.2 = ((bf16[8,64,128]{2,1,0:T(8,128)(2,1)}), bf16[8,64,128]{2,1,0:T(8,128)(2,1)S(1)}, u32[]{:S(2)}, u32[]{:S(2)}) async-start(bf16[8,64,128]{2,1,0:T(8,128)(2,1)} %convolution_convert_fusion), calls=%async_computation.2 | async-start | bytes 262144 | tf_op jit(solution)/shard_map/all_to_all | solution.py:159
Sparse Core Ops, SparseCore 0:
  68.8 14.2 all-gather.6
  99.9 16.6 all-gather.8
